TPU v7x, 128 devices: a whole 4x4x4 slice. The times are simulated.
128 devices in a mesh: batch: 4 (over z_hi, core), centers: 32 (over x, y, z_lo).
Axes of the slice: x: 4, y: 4, z: 4 (z_hi: 2, z_lo: 2; z = z_hi * 2 + z_lo), core: 2. Of those that a mesh axis runs over, the one named last changes fastest.
Arguments:
- pool_features: float32 [131072, 128], P(('batch', 'centers')), may hold values from -14 to 14
- pool_targets: float32 [131072, 64], P(('batch', 'centers')), may hold values from -6 to 6
- batch_index: int32 [8192], P(('batch', 'centers')), may hold values from 0 to 1023
- centers: float32 [16384, 128], P('centers'), may hold values from -14 to 14
- weights: float32 [16384, 64], P('centers'), as said below
- eig_vectors: float32 [16384, 1024], P(('batch', 'centers')), may hold values from -0.046875 to 0.046875
- eig_scale: float32 [1024], replicated, may hold values from 0.5 to 4
- nys_owner: int32 [16384, 1], P(('batch', 'centers')), may hold values from 0 to 31; in each aligned block of 128 rows (0 to 127, 128 to 255, ...) at most 8 rows name the same one
- nys_offset: int32 [16384], P(('batch', 'centers')), may hold values from 0 to 511
Outputs:
- residual_out: float32 [8192, 64], P(('batch', 'centers'))
- update: float32 [16384, 64], P('centers')
Inputs may be any that keep to these rules, and one draw needn't show every extreme that they name: `nys_owner`: among the 128 rows of one device no owner is named more than 8 times; on some devices one owner is named exactly 8 times. `weights`: every column sums to zero.
All inputs are finite; a program needn't handle non-finite values.
Results may differ from a plain program's by a relative error of at most 0.0003.
Values sent between devices are 32-bit elements; how exact they have to be, the bound alone decides.
No kernel may reach another device: no remote copies, remote signals or barrier semaphores. Data moves between devices by JAX's collectives and lax.ppermute only.
A program may use at most 64 MiB of HBM per device.

v0:
```python
import math
import jax
import jax.numpy as jnp
from jax import lax
from jax.sharding import PartitionSpec as P

DEPTH = 3
epsilon = 1e-06
highest = lax.Precision.HIGHEST


def kernel_rows(row_block, center_block, center_norm):
    inner_prod = (
        lax.dot_general(
            row_block,
            center_block,
            (((1,), (1,)), ((), ())),
            precision=highest,
            preferred_element_type=jnp.float32,
        )
        / row_block.shape[1]
    )
    row_norm = jnp.mean(row_block * row_block, axis=1) + epsilon
    norm_scale = jnp.sqrt(row_norm[:, None] * center_norm[None, :])
    sigma_now = inner_prod
    tangent = inner_prod
    for depth_step in range(DEPTH):
        cosine = sigma_now / norm_scale
        arc_angle = jnp.arccos(cosine)
        remain = (math.pi - arc_angle) / math.pi
        sigma_now = (
            norm_scale
            * (jnp.sqrt(1.0 - cosine * cosine) + (math.pi - arc_angle) * cosine)
            / math.pi
        )
        tangent = sigma_now + tangent * remain
    return tangent


def per_device(
    pool_features,
    pool_targets,
    batch_index,
    centers,
    weights,
    eig_vectors,
    eig_scale,
    nys_owner,
    nys_offset,
):
    local_rows = pool_features[batch_index]
    local_targets = pool_targets[batch_index]
    row_count = local_rows.shape[0]
    group_size = lax.axis_size("centers")
    rows_total = row_count * group_size * lax.axis_size("batch")
    center_count = centers.shape[0]
    outputs = weights.shape[1]
    center_norm = jnp.mean(centers * centers, axis=1) + epsilon
    kernel = kernel_rows(
        lax.all_gather(local_rows, "centers", axis=0, tiled=True), centers, center_norm
    )
    partial_pred = jnp.dot(kernel, weights, precision=highest, preferred_element_type=jnp.float32)
    all_targets = lax.all_gather(local_targets, "centers", axis=0, tiled=True)
    prediction = lax.psum(partial_pred, "centers")
    residual = prediction - all_targets
    own_residual = lax.dynamic_slice_in_dim(
        residual, lax.axis_index("centers") * row_count, row_count, 0
    )
    grads_part = lax.dot_general(
        kernel,
        residual,
        (((0,), (0,)), ((), ())),
        precision=highest,
        preferred_element_type=jnp.float32,
    ) / math.sqrt(rows_total)
    grads = lax.psum(grads_part, "batch")
    owner = nys_owner[:, 0]
    slots = max(2, 2 * owner.shape[0] // group_size)
    owner_hot = (owner[:, None] == jnp.arange(group_size, dtype=jnp.int32)[None, :]).astype(
        jnp.int32
    )
    slot_rank = jnp.sum((jnp.cumsum(owner_hot, axis=0) - owner_hot) * owner_hot, axis=1)
    requests = jnp.zeros((group_size, slots), jnp.int32).at[owner, slot_rank].set(nys_offset)
    received = lax.all_to_all(requests, "centers", split_axis=0, concat_axis=0, tiled=True)
    found = grads[received]
    returned = lax.all_to_all(found, "centers", split_axis=0, concat_axis=0, tiled=True)
    picked_grads = returned[owner, slot_rank]
    coeff_part = lax.dot_general(
        eig_vectors,
        picked_grads,
        (((0,), (0,)), ((), ())),
        precision=highest,
        preferred_element_type=jnp.float32,
    )
    coeff = lax.psum(coeff_part, ("batch", "centers"))
    corr_rows = jnp.dot(
        eig_vectors,
        eig_scale[:, None] * coeff,
        precision=highest,
        preferred_element_type=jnp.float32,
    )
    spread = (
        jnp.zeros((group_size * center_count, outputs), jnp.float32)
        .at[owner * center_count + nys_offset]
        .add(corr_rows)
    )
    corr_part = lax.psum_scatter(spread, "centers", scatter_dimension=0, tiled=True)
    correction = lax.psum(corr_part, "batch")
    return (own_residual, correction - grads)


def solution(mesh):
    placed = (
        P(("batch", "centers"), None),
        P(("batch", "centers"), None),
        P(("batch", "centers")),
        P("centers", None),
        P("centers", None),
        P(("batch", "centers"), None),
        P(),
        P(("batch", "centers"), None),
        P(("batch", "centers")),
    )
    return jax.shard_map(
        per_device,
        mesh=mesh,
        in_specs=placed,
        out_specs=(P(("batch", "centers"), None), P("centers", None)),
        check_vma=False,
    )
```

profile of v0, /device:TPU:1, one launch (start us, length us, event | category | flops | bytes accessed | tf_op | source)
XLA Modules:
  0.0 951.3 jit_solution(6418293287864881805)
XLA Ops:
  7.9 2.2 gather_fusion
  11.2 1.1 multiply_reduce_fusion.1
  12.3 130.2 %all-gather.4.cloned.1.call-done = f32[2048,128]{1,0:T(8,128)} async-done(((f32[64,128]{1,0:T(8,128)}), f32[2048,128]{1,0:T(8,128)}) %all-gather.4.cloned.1.call-update) | async-done | bytes 1048592 | tf_op jit(solution)/shard_map/all_gather | solution.py:60
  142.5 1.6 multiply_reduce_fusion
  144.1 37.0 %multiply_add_fusion = f32[2048,512]{1,0:T(8,128)S(1)} fusion(f32[2048,128]{1,0:T(8,128)} %all-gather.4.cloned.1.call-done, f32[512,128]{1,0:T(8,128)} %param.12, f32[512]{0:T(512)S(1)} %multiply_add_fusion.2, f32[2048]{0:T(1024)S(1)} %multiply_add_fusion.1), kind=kOutput, calls=%fused_computation.8 | convolution fusion | flops 1656750080 | bytes 5515264 | tf_op jit(solution)/shard_map/dot_general | solution.py:14
  181.1 1.9 copy-done.1
  183.0 5.0 fusion.8
  188.2 6.4 scatter_fusion
  195.4 6.9 all-to-all-start
  203.2 73.5 %all-gather.1 = f32[2048,64]{1,0:T(8,128)S(1)} all-gather(f32[64,64]{1,0:T(8,128)S(1)} %gather_fusion.1), channel_id=3, replica_groups=mesh['batch'=4,'centers'=32] {'centers'}, dimensions={0}, use_global_device_ids=true | all-gather | bytes 540672 | tf_op jit(solution)/shard_map/all_gather | solution.py:63
  277.0 218.7 %all-reduce.5.cloned.1.call-done = f32[2048,64]{0,1:T(8,128)} async-done(((f32[2048,64]{0,1:T(8,128)}), f32[2048,64]{0,1:T(8,128)}) %all-reduce.5.cloned.1.call-update) | async-done | bytes 524304 | tf_op jit(solution)/shard_map/psum | solution.py:64
  495.7 1.1 sub.36
  496.9 5.6 convolution_multiply_fusion
  502.7 62.1 %all-reduce.7.cloned.1.call-done = f32[512,64]{0,1:T(8,128)} async-done(((f32[512,64]{0,1:T(8,128)}), f32[512,64]{0,1:T(8,128)}) %all-reduce.7.cloned.1.call-update) | async-done | bytes 131088 | tf_op jit(solution)/shard_map/psum | solution.py:76
  564.8 1.0 copy.27
  566.7 13.8 %all_to_all.17 = f32[32,1,512]{2,1,0:T(1,128)S(1)} all-to-all(f32[32,1,512]{2,1,0:T(1,128)S(1)} %reshape.108), channel_id=1, replica_groups=mesh['batch'=4,'centers'=32] {'centers'}, dimensions={0} | all-to-all | bytes 131072 | tf_op jit(solution)/shard_map/all_to_all | solution.py:86
  582.9 1.1 convolution_bitcast_fusion
  584.1 139.3 %all-reduce.9.cloned.1.call-done = f32[1024,64]{0,1:T(8,128)} async-done(((f32[1024,64]{0,1:T(8,128)}), f32[1024,64]{0,1:T(8,128)}) %all-reduce.9.cloned.1.call-update) | async-done | bytes 262160 | tf_op jit(solution)/shard_map/psum | solution.py:95
  723.5 1.6 convolution_bitcast_fusion.1
  725.2 4.7 scatter_custom_fusion.1
  729.9 6.8 copy.29
  736.8 143.0 %reduce-scatter.2.cloned.1.call-done = f32[512,64]{0,1:T(8,128)} async-done(((f32[16384,64]{0,1:T(8,128)}), f32[512,64]{0,1:T(8,128)}) %reduce-scatter.2.cloned.1.call-update) | async-done | bytes 131088 | tf_op jit(solution)/shard_map/reduce_scatter | solution.py:107
  880.6 62.3 %all-reduce.11.cloned.1.call-done = f32[512,64]{0,1:T(8,128)} async-done(((f32[512,64]{0,1:T(8,128)}), f32[512,64]{0,1:T(8,128)}) %all-reduce.11.cloned.1.call-update) | async-done | bytes 131088 | tf_op jit(solution)/shard_map/psum | solution.py:108
  942.9 1.6 sub.38
  (54 shorter events, 8.2 us)
Async XLA Ops:
  7.2 575.7 %copy-start = (f32[128,1024]{1,0:T(8,128)S(1)}, f32[128,1024]{1,0:T(8,128)}, u32[]{:S(2)}) copy-start(f32[128,1024]{1,0:T(8,128)} %param.14) | copy-start | bytes 1572868
  7.2 135.3 %all-gather.4.cloned.1.call-start = ((), (), s32[]{:S(2)}) async-start(), calls=%async_computation.8 | async-start | bytes 1081344 | tf_op jit(solution)/shard_map/all_gather | solution.py:60
  10.2 485.5 %all-reduce.5.cloned.1.call-start = ((), (), s32[]{:S(2)}) async-start(), calls=%async_computation.3 | async-start | bytes 1048576 | tf_op jit(solution)/shard_map/psum | solution.py:64
  144.1 38.9 %copy-start.4 = (f32[512,64]{0,1:T(8,128)S(1)}, f32[512,64]{0,1:T(8,128)}, u32[]{:S(2)}) copy-start(f32[512,64]{0,1:T(8,128)} %param.13) | copy-start | bytes 393220
  181.0 1.9 copy-start.1
  183.0 5.0 copy-start.5
  183.0 5.3 copy-start.7
  183.0 19.4 %copy-start.3 = (f32[1024,64]{0,1:T(8,128)S(1)}, f32[1024,64]{0,1:T(8,128)}, u32[]{:S(2)}) copy-start(f32[1024,64]{0,1:T(8,128)} %param.10) | copy-start | bytes 786436
  195.4 307.2 %all-to-all-start = ((s32[32,1,8]{2,1,0:T(1,128)}), s32[32,1,8]{2,1,0:T(1,128)S(1)}, u32[]{:S(2)}, u32[]{:S(2)}) async-start(s32[32,1,8]{2,1,0:T(1,128)} %copy.26), calls=%async_computation | async-start | bytes 32768 | tf_op jit(solution)/shard_map/all_to_all | solution.py:84
  202.3 362.5 %all-reduce.7.cloned.1.call-start = ((), (), s32[]{:S(2)}) async-start(), calls=%async_computation.4 | async-start | bytes 262144 | tf_op jit(solution)/shard_map/psum | solution.py:76
  496.9 226.6 %copy-start.6 = (f32[1024]{0:T(1024)S(1)}, f32[1024]{0:T(1024)}, u32[]{:S(2)}) copy-start(f32[1024]{0:T(1024)} %param.15) | copy-start | bytes 12292
  502.5 221.0 %all-reduce.9.cloned.1.call-start = ((), (), s32[]{:S(2)}) async-start(), calls=%async_computation.5 | async-start | bytes 524288 | tf_op jit(solution)/shard_map/psum | solution.py:95
  584.1 295.7 %reduce-scatter.2.cloned.1.call-start = ((), (), s32[]{:S(2)}) async-start(), calls=%async_computation.6 | async-start | bytes 4325376 | tf_op jit(solution)/shard_map/reduce_scatter | solution.py:107
  736.7 206.1 %copy-start.2 = (f32[512,64]{0,1:T(8,128)S(1)}, f32[512,64]{0,1:T(8,128)}, u32[]{:S(2)}) copy-start(f32[512,64]{0,1:T(8,128)} %all-reduce.7.cloned.1.call-done) | copy-start | bytes 393220
  736.7 206.1 %all-reduce.11.cloned.1.call-start = ((), (), s32[]{:S(2)}) async-start(), calls=%async_computation.7 | async-start | bytes 262144 | tf_op jit(solution)/shard_map/psum | solution.py:108
Sparse Core Ops, SparseCore 0:
  10.3 132.1 all-gather.3
  188.1 307.5 all-reduce.4
  502.6 62.1 all-reduce.6
  584.2 139.2 all-reduce.8
  736.9 142.8 reduce-scatter.1
  882.1 60.7 all-reduce.10
where the time goes:
time: 952 us; the launch traced here: 951 us
  waiting for transfers between devices  756 us (79%)
  blocking collectives  87.4 us (9%)
  matrix products  50.3 us (5%)
  local copies, waits for them, and re-layouts  23.6 us (2%)
  between operations  14.3 us (2%)
  other arithmetic  12.7 us (1%)
    psum x1, waiting for transfers between devices, per_device(): prediction = lax.psum(partial_pred, 'centers')  219 us
    reduce_scatter x1, waiting for transfers between devices, per_device(): lax.psum_scatter(spread, 'centers', scatter_dimension=0, tiled=True)  143 us
    psum x1, waiting for transfers between devices, per_device(): coeff = lax.psum(coeff_part, ('batch', 'centers'))  139 us
    all_gather x1, waiting for transfers between devices, per_device(): lax.all_gather(local_rows, 'centers', axis=0, tiled=True)  130 us
    all_gather x1, blocking collectives, per_device(): all_targets = lax.all_gather(local_targets, 'centers', axis=0, tiled=True)  73.5 us
    psum x1, waiting for transfers between devices, per_device(): correction = lax.psum(corr_part, 'batch')  62.3 us
    psum x1, waiting for transfers between devices, per_device(): grads = lax.psum(grads_part, 'batch')  62.1 us
    dot_general x1, matrix products, kernel_rows(): lax.dot_general(row_block, center_block, (((1,), (1,)), ((), ())), precis...  37 us
  transfers between devices with their start and end apart: 7, of which 6 were waited for; matrix products, arithmetic and copies ran while one was open for 2% of the time, Pallas kernels for 0%

commit v1 on v0

--- a/solution.py
+++ b/solution.py
@@ -1,3 +1,4 @@
+import functools
 import math
 import jax
 import jax.numpy as jnp
@@ -7,6 +8,13 @@
 DEPTH = 3
 epsilon = 1e-06
 highest = lax.Precision.HIGHEST
+
+
+def reach_domain(unit, axis_tag):
+    return lax.all_gather(unit, axis_tag).sum(axis=0)
+
+
+balance_views = functools.partial(reach_domain, axis_tag="centers")
 
 
 def kernel_rows(row_block, center_block, center_norm):
@@ -61,7 +69,7 @@
     )
     partial_pred = jnp.dot(kernel, weights, precision=highest, preferred_element_type=jnp.float32)
     all_targets = lax.all_gather(local_targets, "centers", axis=0, tiled=True)
-    prediction = lax.psum(partial_pred, "centers")
+    prediction = balance_views(partial_pred)
     residual = prediction - all_targets
     own_residual = lax.dynamic_slice_in_dim(
         residual, lax.axis_index("centers") * row_count, row_count, 0

time: 952 us -> 1050 us (1.10)
  waiting for transfers between devices: 756 us -> 813 us
  local copies, waits for them, and re-layouts: 23.6 us -> 42.3 us
  blocking collectives: 87.4 us -> 104 us
    all_gather x0 -> x1, waiting for transfers between devices: none -> 296 us  [reach_domain(): return lax.all_gather(unit, axis_tag).sum(axis=0)]
    psum x1 -> x0, waiting for transfers between devices: 219 us -> none  [per_device(): prediction = lax.psum(partial_pred, 'centers')]
    psum x1, waiting for transfers between devices: 62.1 us -> 41.5 us  [per_device(): grads = lax.psum(grads_part, 'batch')]
    unnamed x20, local copies, waits for them, and re-layouts: 3.06 us -> 20.2 us
    all_gather x1, blocking collectives: 73.5 us -> 90.6 us  [per_device(): all_targets = lax.all_gather(local_targets, 'centers', axis=0, tiled=True)]
  transfers between devices with their start and end apart: 7 -> 7, of which waited for: 6 -> 6; matrix products, arithmetic and copies ran while one was open for 2% -> 4% of each run, Pallas kernels for 0% -> 0%
where the time goes in v1:
time: 1050 us
  waiting for transfers between devices  813 us (77%)
  blocking collectives  104 us (10%)
  matrix products  50 us (5%)
  local copies, waits for them, and re-layouts  42.3 us (4%)
  other arithmetic  21.1 us (2%)
  between operations  14.3 us (1%)
    all_gather x1, waiting for transfers between devices, reach_domain(): return lax.all_gather(unit, axis_tag).sum(axis=0)  296 us
    reduce_scatter x1, waiting for transfers between devices, per_device(): lax.psum_scatter(spread, 'centers', scatter_dimension=0, tiled=True)  143 us
    psum x1, waiting for transfers between devices, per_device(): coeff = lax.psum(coeff_part, ('batch', 'centers'))  139 us
    all_gather x1, waiting for transfers between devices, per_device(): lax.all_gather(local_rows, 'centers', axis=0, tiled=True)  131 us
    all_gather x1, blocking collectives, per_device(): all_targets = lax.all_gather(local_targets, 'centers', axis=0, tiled=True)  90.6 us
    psum x1, waiting for transfers between devices, per_device(): correction = lax.psum(corr_part, 'batch')  62.5 us
    psum x1, waiting for transfers between devices, per_device(): grads = lax.psum(grads_part, 'batch')  41.5 us
    dot_general x1, matrix products, kernel_rows(): lax.dot_general(row_block, center_block, (((1,), (1,)), ((), ())), precis...  37 us
  transfers between devices with their start and end apart: 7, of which 6 were waited for; matrix products, arithmetic and copies ran while one was open for 4% of the time, Pallas kernels for 0%

profile of v1, /device:TPU:1, one launch (start us, length us, event | category | flops | bytes accessed | tf_op | source)
XLA Modules:
  0.0 1052.7 jit_solution(9933725225812370396)
XLA Ops:
  7.9 2.2 gather_fusion
  11.4 131.1 %all-gather.6.cloned.1.call-done = f32[2048,128]{1,0:T(8,128)} async-done(((f32[64,128]{1,0:T(8,128)}), f32[2048,128]{1,0:T(8,128)}) %all-gather.6.cloned.1.call-update) | async-done | bytes 1048592 | tf_op jit(solution)/shard_map/all_gather | solution.py:68
  142.5 1.6 multiply_reduce_fusion
  144.1 37.0 %multiply_add_fusion = f32[2048,512]{1,0:T(8,128)S(1)} fusion(f32[2048,128]{1,0:T(8,128)} %all-gather.6.cloned.1.call-done, f32[512,128]{1,0:T(8,128)} %param.12, f32[512]{0:T(512)S(1)} %multiply_add_fusion.2, f32[2048]{0:T(1024)S(1)} %multiply_add_fusion.1), kind=kOutput, calls=%fused_computation.9 | convolution fusion | flops 1656750080 | bytes 5515264 | tf_op jit(solution)/shard_map/dot_general | solution.py:22
  181.1 2.0 copy-done.1
  183.1 5.0 fusion.8
  188.6 6.4 scatter_fusion
  195.7 7.0 all-to-all-start
  203.6 90.6 %all-gather.2 = f32[2048,64]{1,0:T(8,128)S(1)} all-gather(f32[64,64]{1,0:T(8,128)S(1)} %gather_fusion.1), channel_id=4, replica_groups=mesh['batch'=4,'centers'=32] {'centers'}, dimensions={0}, use_global_device_ids=true | all-gather | bytes 540672 | tf_op jit(solution)/shard_map/all_gather | solution.py:71
  294.2 296.1 %all-gather.8.cloned.1.call-done = f32[65536,64]{0,1:T(8,128)} async-done(((f32[2048,64]{0,1:T(8,128)}), f32[65536,64]{0,1:T(8,128)}) %all-gather.8.cloned.1.call-update) | async-done | bytes 16777232 | tf_op jit(solution)/shard_map/all_gather | solution.py:14
  590.3 17.7 %copy.26 = f32[8,8,32,2048]{3,2,1,0:T(8,128)} copy(f32[8,8,32,2048]{3,1,2,0:T(8,128)} %bitcast.36) | data formatting | bytes 33554432
  608.0 8.8 bitcast_reduce_fusion
  616.8 1.3 copy.21
  618.1 1.4 sub.36
  619.5 5.3 convolution_multiply_fusion
  625.0 41.5 %all-reduce.4.cloned.1.call-done = f32[512,64]{0,1:T(8,128)} async-done(((f32[512,64]{0,1:T(8,128)}), f32[512,64]{0,1:T(8,128)}) %all-reduce.4.cloned.1.call-update) | async-done | bytes 131088 | tf_op jit(solution)/shard_map/psum | solution.py:84
  668.4 13.8 %all_to_all.17 = f32[32,1,512]{2,1,0:T(1,128)S(1)} all-to-all(f32[32,1,512]{2,1,0:T(1,128)S(1)} %reshape.109), channel_id=1, replica_groups=mesh['batch'=4,'centers'=32] {'centers'}, dimensions={0} | all-to-all | bytes 131072 | tf_op jit(solution)/shard_map/all_to_all | solution.py:94
  686.1 139.1 %all-reduce.6.cloned.1.call-done = f32[1024,64]{0,1:T(8,128)} async-done(((f32[1024,64]{0,1:T(8,128)}), f32[1024,64]{0,1:T(8,128)}) %all-reduce.6.cloned.1.call-update) | async-done | bytes 262160 | tf_op jit(solution)/shard_map/psum | solution.py:103
  825.2 1.6 convolution_bitcast_fusion.1
  826.9 4.7 scatter_custom_fusion.1
  831.6 6.8 copy.25
  838.5 142.6 %reduce-scatter.2.cloned.1.call-done = f32[512,64]{0,1:T(8,128)} async-done(((f32[16384,64]{0,1:T(8,128)}), f32[512,64]{0,1:T(8,128)}) %reduce-scatter.2.cloned.1.call-update) | async-done | bytes 131088 | tf_op jit(solution)/shard_map/reduce_scatter | solution.py:115
  981.7 62.5 %all-reduce.8.cloned.1.call-done = f32[512,64]{0,1:T(8,128)} async-done(((f32[512,64]{0,1:T(8,128)}), f32[512,64]{0,1:T(8,128)}) %all-reduce.8.cloned.1.call-update) | async-done | bytes 131088 | tf_op jit(solution)/shard_map/psum | solution.py:116
  1044.3 1.6 sub.38
  (55 shorter events, 10.5 us)
Async XLA Ops:
  7.2 677.5 %copy-start = (f32[128,1024]{1,0:T(8,128)S(1)}, f32[128,1024]{1,0:T(8,128)}, u32[]{:S(2)}) copy-start(f32[128,1024]{1,0:T(8,128)} %param.14) | copy-start | bytes 1572868
  7.2 135.3 %all-gather.6.cloned.1.call-start = ((), (), s32[]{:S(2)}) async-start(), calls=%async_computation.7 | async-start | bytes 1081344 | tf_op jit(solution)/shard_map/all_gather | solution.py:68
  10.2 580.1 %all-gather.8.cloned.1.call-start = ((), (), s32[]{:S(2)}) async-start(), calls=%async_computation.8 | async-start | bytes 17301504 | tf_op jit(solution)/shard_map/all_gather | solution.py:14
  144.1 39.0 %copy-start.4 = (f32[512,64]{0,1:T(8,128)S(1)}, f32[512,64]{0,1:T(8,128)}, u32[]{:S(2)}) copy-start(f32[512,64]{0,1:T(8,128)} %param.13) | copy-start | bytes 393220
  181.1 2.0 copy-start.1
  183.1 5.0 copy-start.5
  183.1 5.5 copy-start.7
  183.1 19.6 %copy-start.3 = (f32[1024,64]{0,1:T(8,128)S(1)}, f32[1024,64]{0,1:T(8,128)}, u32[]{:S(2)}) copy-start(f32[1024,64]{0,1:T(8,128)} %param.10) | copy-start | bytes 786436
  195.7 429.1 %all-to-all-start = ((s32[32,1,8]{2,1,0:T(1,128)}), s32[32,1,8]{2,1,0:T(1,128)S(1)}, u32[]{:S(2)}, u32[]{:S(2)}) async-start(s32[32,1,8]{2,1,0:T(1,128)} %copy.22), calls=%async_computation | async-start | bytes 32768 | tf_op jit(solution)/shard_map/all_to_all | solution.py:92
  202.7 463.8 %all-reduce.4.cloned.1.call-start = ((), (), s32[]{:S(2)}) async-start(), calls=%async_computation.3 | async-start | bytes 262144 | tf_op jit(solution)/shard_map/psum | solution.py:84
  619.5 205.7 %copy-start.6 = (f32[1024]{0:T(1024)S(1)}, f32[1024]{0:T(1024)}, u32[]{:S(2)}) copy-start(f32[1024]{0:T(1024)} %param.15) | copy-start | bytes 12292
  624.8 200.3 %all-reduce.6.cloned.1.call-start = ((), (), s32[]{:S(2)}) async-start(), calls=%async_computation.4 | async-start | bytes 524288 | tf_op jit(solution)/shard_map/psum | solution.py:103
  685.8 295.3 %reduce-scatter.2.cloned.1.call-start = ((), (), s32[]{:S(2)}) async-start(), calls=%async_computation.5 | async-start | bytes 4325376 | tf_op jit(solution)/shard_map/reduce_scatter | solution.py:115
  838.4 205.9 %copy-start.2 = (f32[512,64]{0,1:T(8,128)S(1)}, f32[512,64]{0,1:T(8,128)}, u32[]{:S(2)}) copy-start(f32[512,64]{0,1:T(8,128)} %all-reduce.4.cloned.1.call-done) | copy-start | bytes 393220
  838.4 205.8 %all-reduce.8.cloned.1.call-start = ((), (), s32[]{:S(2)}) async-start(), calls=%async_computation.6 | async-start | bytes 262144 | tf_op jit(solution)/shard_map/psum | solution.py:116
Sparse Core Ops, SparseCore 0:
  10.3 132.1 all-gather.5
  188.2 402.0 all-gather.7
  624.9 41.5 all-reduce.3
  685.9 139.1 all-reduce.5
  838.6 142.4 reduce-scatter.1
  983.6 60.6 all-reduce.7
